TPU v7x, 256 devices: a whole 4x4x8 slice. The times are simulated.
256 devices in a mesh: subset: 64 (over x, z, core), vocab: 4 (over y).
Axes of the slice: x: 4, y: 4, z: 8, core: 2. Of those that a mesh axis runs over, the one named last changes fastest.
Arguments:
- hidden: bfloat16 [32768, 2048], P('subset', 'vocab'), may hold values from -100 to 100
- proj_weight: bfloat16 [2048, 25600], P('subset', 'vocab'), may hold values from -1 to 1
- targets: int32 [32768], P('subset'), may hold values from 0 to 25599
- counts: int32 [64, 100, 512], P('subset', 'vocab'), may hold values from 1 to 127, as said below
- ranks: int32 [8], replicated, may hold values from 0 to 6399
Outputs:
- row_cross_entropy: float32 [32768], P('subset')
- resample_mean_losses: float32 [64, 100], P('subset', 'vocab')
- quantiles: float32 [8], replicated
Inputs may be any that keep to these rules, and one draw needn't show every extreme that they name: For every subset and resample the counts over the 512 rows sum to 32768.
All inputs are finite; a program needn't handle non-finite values.
Results may differ from a plain program's by a relative error of at most 0.0003.
Values may be sent and summed in bfloat16 or wider, within the bound.
A program may use at most 128 MiB of HBM per device.

v0:
```python
import jax
import jax.numpy as jnp
from jax import lax
from jax.sharding import PartitionSpec as P


def copy_for_each(value, axis):
    copies = jnp.broadcast_to(value, (lax.axis_size(axis), *value.shape))
    return lax.all_to_all(copies, axis, split_axis=0, concat_axis=0, tiled=True)


def in_order(tiles, dim):
    tiles = jnp.moveaxis(tiles, 0, dim)
    dims = tiles.shape
    return tiles.reshape(*dims[:dim], dims[dim] * dims[dim + 1], *dims[dim + 2 :])


def gathered_copies(value, axis, dim):
    tiles = copy_for_each(value, axis)
    return in_order(tiles, dim)


def gathered_once(value, axis):
    leaves = jax.tree.leaves(value)
    turns = sorted(range(len(leaves)), key=lambda k: -leaves[k].size)
    width = (1, *leaves[turns[0]].shape)[-1]
    lines = [
        jnp.pad(leaves[k].reshape(-1), (0, -leaves[k].size % width)).reshape(-1, width)
        for k in turns
    ]
    both, at, found = (copy_for_each(jnp.concatenate(lines), axis), 0, {})
    for k, line in zip(turns, lines):
        slab = both[:, at : at + len(line)].reshape(len(both), -1)
        found[k] = slab[:, : leaves[k].size].reshape(-1, *leaves[k].shape)
        at += len(line)
    numbers = iter(range(len(leaves)))
    return jax.tree.map(lambda _: found[next(numbers)], value)


def combined_pairwise(pieces, combine):
    while len(jax.tree.leaves(pieces)[0]) > 1:
        pieces = jax.vmap(combine)(
            *(jax.tree.map(lambda part: part[side::2], pieces) for side in (0, 1))
        )
    return jax.tree.map(lambda part: part[0], pieces)


def joined_all(value, axis, combine):
    pieces = gathered_once(value, axis)
    return combined_pairwise(pieces, combine)


def combine_stats(first, second):
    merged_top = jnp.maximum(first[0], second[0])
    merged_sum = first[1] * jnp.exp(first[0] - merged_top) + second[1] * jnp.exp(
        second[0] - merged_top
    )
    return (merged_top, merged_sum, first[2] + second[2])


def shards(hidden, proj_weight, targets, counts, ranks):
    features = gathered_copies(hidden, "vocab", 1)
    columns = proj_weight.shape[1]
    whole_weight = lax.all_gather(proj_weight, "subset", axis=0, tiled=True)
    logit_scores = jnp.dot(features, whole_weight, preferred_element_type=jnp.float32)
    local_top = jnp.max(logit_scores, axis=1)
    local_sum = jnp.sum(jnp.exp(logit_scores - local_top[:, None]), axis=1)
    offset = targets - lax.axis_index("vocab") * columns
    inside = (offset >= 0) & (offset < columns)
    picked = jnp.take_along_axis(logit_scores, jnp.clip(offset, 0, columns - 1)[:, None], axis=1)[
        :, 0
    ]
    picked = jnp.where(inside, picked, 0.0)
    row_max, row_total, target_logit = joined_all(
        (local_top, local_sum, picked), "vocab", combine_stats
    )
    row_cross_entropy = row_max + jnp.log(row_total) - target_logit
    total_rows = 1.0 * lax.axis_size("subset") * row_cross_entropy.shape[0]
    resample_mean_losses = (
        jnp.einsum(
            "cno,o->cn",
            counts.astype(jnp.float32),
            row_cross_entropy,
            precision=lax.Precision.HIGHEST,
        )
        / total_rows
    )
    grouped = gathered_copies(resample_mean_losses, "vocab", 1)
    gathered = gathered_copies(grouped, "subset", 0)
    pooled = jnp.sort(gathered.reshape(-1))
    positions = lax.iota(jnp.int32, pooled.shape[0])
    chosen = positions[:, None] == ranks[None, :]
    quantiles = jnp.sum(jnp.where(chosen, pooled[:, None], 0.0), axis=0)
    return (row_cross_entropy, resample_mean_losses, quantiles)


def solution(mesh):
    return jax.shard_map(
        shards,
        mesh=mesh,
        in_specs=(
            P("subset", "vocab"),
            P("subset", "vocab"),
            P("subset"),
            P("subset", "vocab", None),
            P(),
        ),
        out_specs=(P("subset"), P("subset", "vocab"), P()),
        check_vma=False,
    )
```

profile of v0, /device:TPU:1, one launch (start us, length us, event | category | flops | bytes accessed | tf_op | source)
XLA Modules:
  0.0 225.7 jit_solution(18324413757719178273)
XLA Ops:
  7.2 0.0 all-gather.2.cloned.1.call-start
  7.2 0.7 all-gather.2.cloned.1.call-update
  7.9 1.3 copy.16
  9.2 1.5 broadcast_in_dim.37
  10.6 5.0 %all-to-all-start = ((bf16[4,512,512]{1,2,0:T(8,128)(2,1)}), bf16[4,512,512]{1,2,0:T(8,128)(2,1)S(1)}, u32[]{:S(2)}, u32[]{:S(2)}) async-start(bf16[4,512,512]{1,2,0:T(8,128)(2,1)} %broadcast_in_dim.37), calls=%async_computation | async-start | bytes 4194304 | tf_op jit(solution)/shard_map/all_to_all | solution.py:9
  15.7 0.7 compare_select_fusion
  16.4 23.8 %all-to-all-done = bf16[4,512,512]{1,2,0:T(8,128)(2,1)S(1)} async-done(((bf16[4,512,512]{1,2,0:T(8,128)(2,1)}), bf16[4,512,512]{1,2,0:T(8,128)(2,1)S(1)}, u32[]{:S(2)}, u32[]{:S(2)}) %all-to-all-start) | async-done | bytes 2097184 | tf_op jit(solution)/shard_map/all_to_all | solution.py:9
  40.2 98.7 %all-gather.2.cloned.1.call-done = bf16[2048,6400]{1,0:T(8,128)(2,1)} async-done(((bf16[32,6400]{1,0:T(8,128)(2,1)}), bf16[2048,6400]{1,0:T(8,128)(2,1)}) %all-gather.2.cloned.1.call-update) | async-done | bytes 26214416 | tf_op jit(solution)/shard_map/all_gather | solution.py:64
  138.9 22.2 %fusion.11 = (f32[512]{0:T(512)S(1)}, f32[512,6400]{1,0:T(8,128)}) fusion(bf16[512,2048]{0,1:T(8,128)(2,1)S(1)} %bitcast.32, bf16[2048,6400]{1,0:T(8,128)(2,1)} %all-gather.2.cloned.1.call-done), kind=kOutput, calls=%fused_computation.30 | convolution fusion | flops 13425049600 | bytes 41420800 | tf_op jit(solution)/shard_map/dot_general | solution.py:65
  161.0 0.0 copy-start.2
  161.0 0.0 copy-start
  161.0 0.0 copy-start.4
  161.0 6.6 %exponential_reduce_fusion = f32[512]{0:T(512)S(1)} fusion(f32[512,6400]{1,0:T(8,128)} %get-tuple-element.12, f32[512]{0:T(512)S(1)} %get-tuple-element.11), kind=kLoop, calls=%fused_computation.1 | loop fusion | flops 6553088 | bytes 13111296 | tf_op jit(solution)/shard_map/reduce_sum | solution.py:67
  167.7 8.1 %gather_fusion = f32[512]{0:T(512)S(1)} fusion(f32[512,6400]{1,0:T(8,128)} %get-tuple-element.12, s32[512]{0:T(512)S(1)} %bitcast.31), kind=kCustom, calls=%fused_computation | custom fusion | bytes 8192 | tf_op jit(solution)/shard_map/jit(take_along_axis)/gather | solution.py:70
  175.8 0.0 copy-done.2
  175.9 0.6 broadcast_in_dim.40
  176.5 3.7 %all-to-all-start.1 = ((f32[4,3,512]{2,1,0:T(4,128)}), f32[4,3,512]{2,1,0:T(4,128)S(1)}, u32[]{:S(2)}, u32[]{:S(2)}) async-start(f32[4,3,512]{2,1,0:T(4,128)} %broadcast_in_dim.40), calls=%async_computation.1 | async-start | bytes 65536 | tf_op jit(solution)/shard_map/all_to_all | solution.py:9
  180.2 0.0 copy-done
  180.3 4.3 %all-to-all-done.1 = f32[4,3,512]{2,1,0:T(4,128)S(1)} async-done(((f32[4,3,512]{2,1,0:T(4,128)}), f32[4,3,512]{2,1,0:T(4,128)S(1)}, u32[]{:S(2)}, u32[]{:S(2)}) %all-to-all-start.1) | async-done | bytes 24608 | tf_op jit(solution)/shard_map/all_to_all | solution.py:9
  184.8 0.0 copy-start.1
  184.8 0.1 fusion
  184.9 0.0 copy-start.3
  185.0 6.4 %all_to_all.20 = f32[4,1,25]{2,1,0:T(1,128)S(1)} all-to-all(f32[4,1,25]{2,1,0:T(1,128)S(1)} %broadcast_in_dim.41), channel_id=1, replica_groups=mesh['subset'=64,'vocab'=4] {'vocab'}, dimensions={0} | all-to-all | bytes 800 | tf_op jit(solution)/shard_map/all_to_all | solution.py:9
  191.4 0.5 broadcast.54
  191.9 0.7 reduce.6
  192.6 0.1 reshape_transpose.3
  192.7 17.7 %all_to_all.21 = f32[64,1,100]{2,1,0:T(1,128)S(1)} all-to-all(f32[64,1,100]{2,1,0:T(1,128)S(1)} %broadcast_in_dim.42), channel_id=1, replica_groups=mesh['subset'=64,'vocab'=4] {'subset'}, dimensions={0} | all-to-all | bytes 51200 | tf_op jit(solution)/shard_map/all_to_all | solution.py:9
  210.4 0.7 reduce.7
  211.1 0.1 reshape_reshape.3
  211.2 6.9 %sort.15 = (f32[6400]{0:T(1024)S(1)}, s32[6400]{0:T(1024)}) sort(f32[6400]{0:T(1024)S(1)} %reshape_reshape.3, s32[6400]{0:T(1024)S(1)} %iota.7), dimensions={0}, to_apply=%region_2.3 | sort | flops 83200 | bytes 102400 | tf_op jit(solution)/shard_map/jit(sort)/sort | solution.py:90
  218.1 0.0 copy-done.4
  218.1 0.7 select_reduce_fusion
  218.9 0.0 copy-done.1
  218.9 0.0 copy-done.3
  (21 shorter events, 0.4 us)
Async XLA Ops:
  7.2 131.7 %all-gather.2.cloned.1.call-start = ((), (), s32[]{:S(2)}) async-start(), calls=%async_computation.4 | async-start | bytes 26624000 | tf_op jit(solution)/shard_map/all_gather | solution.py:64
  10.6 29.6 %all-to-all-start = ((bf16[4,512,512]{1,2,0:T(8,128)(2,1)}), bf16[4,512,512]{1,2,0:T(8,128)(2,1)S(1)}, u32[]{:S(2)}, u32[]{:S(2)}) async-start(bf16[4,512,512]{1,2,0:T(8,128)(2,1)} %broadcast_in_dim.37), calls=%async_computation | async-start | bytes 4194304 | tf_op jit(solution)/shard_map/all_to_all | solution.py:9
  161.0 14.8 %copy-start.2 = (s32[512]{0:T(512)S(1)}, s32[512]{0:T(512)}, u32[]{:S(2)}) copy-start(s32[512]{0:T(512)} %param.7) | copy-start | bytes 6148
  161.0 19.2 %copy-start = (s32[1,25,512]{2,0,1:T(1,128)S(1)}, s32[1,25,512]{2,0,1:T(1,128)}, u32[]{:S(2)}) copy-start(s32[1,25,512]{2,0,1:T(1,128)} %param.8) | copy-start | bytes 153604
  161.0 57.1 %copy-start.4 = (s32[8]{0:T(128)S(1)}, s32[8]{0:T(128)}, u32[]{:S(2)}) copy-start(s32[8]{0:T(128)} %param.9) | copy-start | bytes 100
  176.5 8.0 %all-to-all-start.1 = ((f32[4,3,512]{2,1,0:T(4,128)}), f32[4,3,512]{2,1,0:T(4,128)S(1)}, u32[]{:S(2)}, u32[]{:S(2)}) async-start(f32[4,3,512]{2,1,0:T(4,128)} %broadcast_in_dim.40), calls=%async_computation.1 | async-start | bytes 65536 | tf_op jit(solution)/shard_map/all_to_all | solution.py:9
  184.8 34.1 %copy-start.1 = (f32[1,512]{1,0:T(1,128)}, f32[1,512]{1,0:T(1,128)S(1)}, u32[]{:S(2)}) copy-start(f32[1,512]{1,0:T(1,128)S(1)} %fusion.3) | copy-start | bytes 6148
  184.9 34.0 %copy-start.3 = (f32[25]{0:T(128)}, f32[25]{0:T(128)S(1)}, u32[]{:S(2)}) copy-start(f32[25]{0:T(128)S(1)} %fusion) | copy-start | bytes 304
Sparse Core Ops, SparseCore 0:
  10.7 128.0 all-gather.1
where the time goes:
time: 226 us
  waiting for transfers between devices  127 us (56%)
  blocking collectives  24.1 us (11%)
  matrix products  22.3 us (10%)
  other arithmetic  16.5 us (7%)
  between operations  14.2 us (6%)
  local copies, waits for them, and re-layouts  12.4 us (5%)
  starting transfers between devices  8.79 us (4%)
    all_gather x1, waiting for transfers between devices, shards(): whole_weight = lax.all_gather(proj_weight, 'subset', axis=0, tiled=True)  98.7 us
    all_to_all x2, waiting for transfers between devices, copy_for_each(): return lax.all_to_all(copies, axis, split_axis=0, concat_axis=0, tiled=True)  28.1 us
    all_to_all x2, blocking collectives, copy_for_each(): return lax.all_to_all(copies, axis, split_axis=0, concat_axis=0, tiled=True)  24.1 us
    dot_general x1, matrix products, shards(): jnp.dot(features, whole_weight, preferred_element_type=jnp.float32)  22.2 us
    all_to_all x2, starting transfers between devices, copy_for_each(): return lax.all_to_all(copies, axis, split_axis=0, concat_axis=0, tiled=True)  8.76 us
    gather x1, local copies, waits for them, and re-layouts, shards(): jnp.take_along_axis(logit_scores, jnp.clip(offset, 0, columns - 1)[:, Non...  8.14 us
    sort x1, other arithmetic, shards(): pooled = jnp.sort(gathered.reshape(-1))  6.9 us
    reduce_sum x1, other arithmetic, shards(): local_sum = jnp.sum(jnp.exp(logit_scores - local_top[:, None]), axis=1)  6.61 us
  transfers between devices with their start and end apart: 3, of which 3 were waited for; matrix products, arithmetic and copies ran while one was open for 2% of the time, Pallas kernels for 0%

commit v1 on v0

v1 whole, which is shorter than its diff:
```python
import jax
import jax.numpy as jnp
from jax import lax
from jax.experimental import pallas as pl
from jax.experimental.pallas import tpu as pltpu
from jax.sharding import PartitionSpec as P

MESH = pl.DeviceIdType.MESH
NX, NY, NZ, NC = 4, 4, 8, 2
ROWS = 512
HALF = 256
QTR = 128
KB = 512
COLS = 6400
TILES = 13
WIDE = TILES * 128
STRIP = 32
RES = 25
ITEMS = 10
ZITEMS = 14
BIG = 3.0e38


def kernel(
    ranks, h_in, w_in, t_in, c_in,
    ce_out, mean_out, q_out,
    hb, wb, acc, mx, ssum, spick, smax, tsub, tbuf, cbuf, cpad, crhs, sbuf, stats, rows1, mine1, rows2, mine2,
    local_sem, xa_send, xa_recv, t_send, t_recv, h_send, h_recv, z_send, z_recv, c_send, c_recv,
    s_send, s_recv, g_send, g_recv, k_send, k_recv,
):
    sub = lax.axis_index("subset")
    y = lax.axis_index("vocab")
    x = sub // (NZ * NC)
    z = (sub // NC) % NZ
    c = sub % NC

    def at(xx, yy, zz, cc):
        return (((xx + NX) % NX) * (NZ * NC) + ((zz + NZ) % NZ) * NC + (cc + NC) % NC, (yy + NY) % NY)

    plane = [(dx, dy) for dx in range(NX) for dy in range(NY) if (dx, dy) != (0, 0)]
    line = [(dz, dc) for dz in range(NZ) for dc in range(NC) if (dz, dc) != (0, 0)]

    def remote(src, dst, ss, rs, dev):
        return pltpu.make_async_remote_copy(
            src_ref=src, dst_ref=dst, send_sem=ss, recv_sem=rs, device_id=dev, device_id_type=MESH
        )

    def local(src, dst, sem):
        return pltpu.make_async_copy(src, dst, sem)

    sends = []

    def start(copy):
        copy.start()
        sends.append(copy)

    own_h = local(h_in, hb.at[x, y], local_sem.at[0])
    own_h.start()

    def colrange(xx):
        return pl.ds(pl.multiple_of(((25 * xx) // 2) * 128, 128), WIDE)

    def strip(zz, cc):
        return pl.ds(pl.multiple_of(zz * (NC * STRIP) + cc * STRIP, STRIP), STRIP)

    own_w = local(w_in.at[:, colrange(x)], wb.at[x, strip(z, c), :], xa_recv.at[0])
    own_w.start()
    own_t = local(t_in, tbuf.at[x], t_recv.at[0])
    own_t.start()
    own_c = local(c_in.at[0], cbuf, local_sem.at[1])
    own_c.start()

    barrier = pltpu.get_barrier_semaphore()
    for dx, dy in plane:
        pl.semaphore_signal(barrier, inc=1, device_id=at(x + dx, y + dy, z, c), device_id_type=MESH)
    for dz, dc in line:
        pl.semaphore_signal(barrier, inc=1, device_id=at(x, y, z + dz, c + dc), device_id_type=MESH)
    pl.semaphore_wait(barrier, len(plane) + len(line))

    for d in (1, 3, 2):
        xx = (x + d) % NX
        start(
            remote(
                w_in.at[:, colrange(xx)], wb.at[x, strip(z, c), :],
                xa_send.at[d], xa_recv.at[(NX - d) % NX], at(xx, y, z, c),
            )
        )

    def wait_cols(q):
        off = (q - x + NX) % NX
        local(w_in.at[:, colrange(0)], wb.at[q, strip(z, c), :], xa_recv.at[off]).wait()

    def span(path, part):
        if part is None:
            return pl.ds(path * HALF, HALF)
        return pl.ds(path * HALF + part * QTR, QTR)

    def place(axis, along, cross, path, part):
        along, cross = (along + 4) % 4, (cross + 4) % 4
        xx, yy = (along, cross) if axis == 0 else (cross, along)
        return hb.at[xx, yy, span(path, part), :]

    def item(axis, d, j, me_along, cross):
        first, second = (0, 1) if axis == 0 else (1, 0)
        part = 0 if d == 1 else 1
        back = me_along - d
        if j == 0:
            return place(axis, me_along, cross, first, None)
        if j == 2:
            return place(axis, back, cross, first, part)
        if j in (1, 3, 5, 7):
            return place(axis, me_along, cross + {1: 0, 3: 1, 5: -1, 7: 2}[j], second, None)
        return place(axis, back, cross + {4: 0, 6: 1, 8: -1, 9: 2}[j], second, part)

    def links():
        for axis in (0, 1):
            for d in (1, -1):
                yield axis, d, 2 * axis + (0 if d == 1 else 1)

    def coords(axis):
        return (x, y) if axis == 0 else (y, x)

    def neighbour(axis, d):
        return at(x + d, y, z, c) if axis == 0 else at(x, y + d, z, c)

    def send_h(j):
        for axis, d, n in links():
            along, cross = coords(axis)
            dst = item(axis, d, j, along, cross)
            first, second = (0, 1) if axis == 0 else (1, 0)
            src = dst
            if j == 0:
                src = h_in.at[span(first, None), :]
            if j == 1:
                src = h_in.at[span(second, None), :]
            start(remote(src, dst, h_send.at[n, j], h_recv.at[n, j], neighbour(axis, d)))

    def wait_h(j):
        for axis, d, n in links():
            along, cross = coords(axis)
            got = item(axis, d, j, along - d, cross)
            remote(got, got, h_send.at[n, j], h_recv.at[n, j], neighbour(axis, d)).wait_recv()

    send_h(0)
    send_h(1)

    for d in (1, 2, 3):
        start(
            remote(t_in, tbuf.at[x], t_send.at[d], t_recv.at[(NX - d) % NX], at(x + d, y, z, c))
        )

    order = [y, (y + 1) % 4, (y + 3) % 4, (y + 2) % 4]

    def zitem(d, j):
        pair, i = divmod(j, 7)
        turn = 0 if d == 1 else 1
        return 2 * pair + (i + turn) % 2, i // 2

    def send_core(o, hops):
        ref = wb.at[order[o], strip((z - hops + NZ) % NZ, c), :]
        n = o * NZ + hops % NZ
        start(remote(ref, ref, c_send.at[n], c_recv.at[n], at(x, y, z, c + 1)))

    def wait_core(o):
        for hops in range(NZ):
            ref = wb.at[order[o], strip((z - hops + NZ) % NZ, (c + 1) % NC), :]
            n = o * NZ + hops
            remote(ref, ref, c_send.at[n], c_recv.at[n], at(x, y, z, c + 1)).wait_recv()

    def send_z(j):
        for i, d in enumerate((1, -1)):
            o, k = zitem(d, j)
            ref = wb.at[order[o], strip((z - d * k + NZ) % NZ, c), :]
            start(remote(ref, ref, z_send.at[i, j], z_recv.at[i, j], at(x, y, z + d, c)))

    def wait_z(j):
        for i, d in enumerate((1, -1)):
            o, k = zitem(d, j)
            ref = wb.at[order[o], strip((z - d * (k + 1) + NZ) % NZ, c), :]
            remote(ref, ref, z_send.at[i, j], z_recv.at[i, j], at(x, y, z + d, c)).wait_recv()
            send_core(o, d * (k + 1))

    def step_z(j):
        wait_z(j)
        if j + 2 < ZITEMS:
            if j + 2 == 7:
                own_cols(2)
                own_cols(3)
            send_z(j + 2)

    def own_cols(o):
        wait_cols(order[o])
        send_core(o, 0)

    own_cols(0)
    own_cols(1)
    send_z(0)
    send_z(1)

    lane = lax.broadcasted_iota(jnp.int32, (ROWS, 128), 1).astype(jnp.float32)
    odd = (x % 2).astype(jnp.float32)
    keep = 1.0 - odd
    away = odd * 1048576.0
    base = (y * COLS + ((25 * x) // 2) * 128).astype(jnp.float32)

    def prepare():
        local(t_in, tbuf.at[x], t_recv.at[0]).wait()
        for d in (1, 2, 3):
            ref = tbuf.at[(x + d) % NX]
            remote(ref, ref, t_send.at[d], t_recv.at[d], at(x + d, y, z, c)).wait_recv()
        for b in range(NX):
            t = tbuf[b].astype(jnp.float32) - base
            tsub[b] = jnp.broadcast_to(t, (128, ROWS)).T - lane
        own_c.wait()
        cpad[...] = jnp.zeros(cpad.shape, jnp.float32)
        cpad[pl.ds(0, RES), :] = cbuf[...].astype(jnp.float32)
        cs = cpad[...].astype(jnp.bfloat16)
        to = lax.broadcasted_iota(jnp.int32, (128, 32), 0)
        frm = lax.broadcasted_iota(jnp.int32, (128, 32), 1)
        for k, shift in ((0, 0), (1, RES * y)):
            move = jnp.where(to == frm + shift, 1.0, 0.0).astype(jnp.bfloat16)
            crhs[pl.ds(k * 128, 128), :] = jnp.dot(
                move, cs, preferred_element_type=jnp.float32
            ).astype(jnp.bfloat16)

    def tile(b, pair, lo, width):
        ka, kb = order[2 * pair], order[2 * pair + 1]
        cols = pl.ds(lo, width)
        return jnp.dot(hb[b, ka], wb[ka, :, cols], preferred_element_type=jnp.float32) + jnp.dot(
            hb[b, kb], wb[kb, :, cols], preferred_element_type=jnp.float32
        )

    def unit(b, pair):
        def put(j, value):
            if pair == 0:
                acc[b, j] = value
            else:
                value = value + acc[b, j]
                acc[b, j] = value
                mx[...] = jnp.maximum(mx[...], value)

        if pair == 1:
            mx[...] = jnp.full(mx.shape, -BIG, jnp.float32)

        @pl.loop(0, TILES // 2)
        def _(n):
            part = tile(b, pair, pl.multiple_of(n * 256, 256), 256)
            put(2 * n, part[:, :128])
            put(2 * n + 1, part[:, 128:])

        put(TILES - 1, tile(b, pair, (TILES - 1) * 128, 128))

    def finish(b):
        @pl.loop(0, ROWS // 64)
        def _(r):
            rows = pl.ds(pl.multiple_of(r * 64, 64), 64)
            top = jnp.max(mx[rows, :], axis=1, keepdims=True)
            top = jnp.broadcast_to(top, (64, 128))
            want = tsub[b, rows, :]
            total = picked = None
            for j in range(TILES):
                value = acc[b, j, rows, :]
                e = jnp.exp(value - top)
                if j == 0:
                    total = e * keep
                    picked = jnp.where(want + away == 0.0, value, 0.0)
                else:
                    total = total + e
                    picked = jnp.where(want == j * 128.0, value, picked)
            smax[rows, :] = top
            ssum[rows, :] = total
            spick[rows, :] = picked

        sbuf[b, pl.ds(0, 1), :] = smax[...].T[:1]
        sbuf[b, pl.ds(1, 1), :] = jnp.sum(ssum[...].T, axis=0, keepdims=True)
        sbuf[b, pl.ds(2, 1), :] = jnp.sum(spick[...].T, axis=0, keepdims=True)
        sbuf[b, pl.ds(3, 1), :] = jnp.zeros((1, ROWS), jnp.float32)

    def send_stats(dx):
        b = (x + dx) % NX
        for dy in range(NY):
            src, dst = sbuf.at[b], stats.at[((NX - dx) % NX) * NY + (NY - dy) % NY]
            n = dx * NY + dy
            if n == 0:
                local(src, dst, s_recv.at[0]).start()
            else:
                m = ((NX - dx) % NX) * NY + (NY - dy) % NY
                start(remote(src, dst, s_send.at[n], s_recv.at[m], at(b, y + dy, z, c)))

    def block(dx):
        return (x + dx) % NX

    wait_h(0)
    send_h(2)
    send_h(3)
    step_z(0)
    step_z(1)
    prepare()
    step_z(2)
    wait_h(1)
    send_h(4)
    step_z(3)
    wait_h(2)
    send_h(5)
    step_z(4)
    step_z(5)
    step_z(6)
    own_h.wait()
    wait_core(0)
    wait_core(1)
    unit(block(0), 0)
    wait_h(3)
    send_h(6)
    step_z(7)
    unit(block(1), 0)
    wait_h(4)
    send_h(7)
    step_z(8)
    step_z(9)
    wait_h(5)
    send_h(8)
    step_z(10)
    unit(block(3), 0)
    step_z(11)
    wait_h(6)
    step_z(12)
    step_z(13)
    wait_core(2)
    wait_core(3)
    unit(block(0), 1)
    finish(block(0))
    send_stats(0)
    wait_h(7)
    send_h(9)
    unit(block(2), 0)
    unit(block(1), 1)
    finish(block(1))
    send_stats(1)
    wait_h(8)
    unit(block(3), 1)
    finish(block(3))
    send_stats(3)
    wait_h(9)
    unit(block(2), 1)
    finish(block(2))
    send_stats(2)

    local(sbuf.at[x], stats.at[0], s_recv.at[0]).wait()
    for n in range(1, NX * NY):
        ref = stats.at[n]
        remote(ref, ref, s_send.at[n], s_recv.at[n], at(x, y, z, c)).wait_recv()
    tops = [stats[n, 0:1, :] for n in range(NX * NY)]
    top = tops[0]
    for t in tops[1:]:
        top = jnp.maximum(top, t)
    total = jnp.zeros((1, ROWS), jnp.float32)
    target = jnp.zeros((1, ROWS), jnp.float32)
    for n in range(NX * NY):
        total = total + stats[n, 1:2, :] * jnp.exp(tops[n] - top)
        target = target + stats[n, 2:3, :]
    ce = top + jnp.log(total) - target
    ce_out[...] = ce

    high = ce.astype(jnp.bfloat16)
    rest = ce - high.astype(jnp.float32)
    middle = rest.astype(jnp.bfloat16)
    low = (rest - middle.astype(jnp.float32)).astype(jnp.bfloat16)
    which = lax.broadcasted_iota(jnp.int32, (16, ROWS), 0)
    pieces = jnp.where(
        which == 0,
        high.astype(jnp.float32),
        jnp.where(which == 1, middle.astype(jnp.float32), jnp.where(which == 2, low.astype(jnp.float32), 0.0)),
    ).astype(jnp.bfloat16)
    sums = lax.dot_general(
        pieces, crhs[...], (((1,), (1,)), ((), ())), preferred_element_type=jnp.float32
    )
    means = jnp.sum(sums, axis=0, keepdims=True) * (1.0 / 32768.0)
    mean_out[...] = means[:, :RES]
    mine1[...] = means[:, 128:]

    for dx, dy in plane:
        n = dx * NY + dy
        m = ((NX - dx) % NX) * NY + (NY - dy) % NY
        start(remote(mine1, rows1.at[m], g_send.at[n], g_recv.at[m], at(x + dx, y + dy, z, c)))
    for dx, dy in plane:
        n = dx * NY + dy
        ref = rows1.at[n]
        remote(ref, ref, g_send.at[n], g_recv.at[n], at(x, y, z, c)).wait_recv()
    for dx in range(NX):
        line_sum = mine1[...] if dx == 0 else rows1[dx * NY]
        for dy in range(1, NY):
            line_sum = line_sum + rows1[dx * NY + dy]
        mine2[pl.ds(dx, 1), :] = line_sum
    for dz, dc in line:
        n = dz * NC + dc
        m = ((NZ - dz) % NZ) * NC + dc
        start(remote(mine2, rows2.at[m], k_send.at[n], k_recv.at[m], at(x, y, z + dz, c + dc)))
    rows2[0] = mine2[...]
    for dz, dc in line:
        n = dz * NC + dc
        ref = rows2.at[n]
        remote(ref, ref, k_send.at[n], k_recv.at[n], at(x, y, z, c)).wait_recv()

    col = lax.broadcasted_iota(jnp.int32, (8, 128), 1)
    rowi = lax.broadcasted_iota(jnp.int32, (8, 128), 0)
    want = jnp.zeros((8, 128), jnp.float32)
    for q in range(8):
        want = jnp.where(rowi == q, ranks[q].astype(jnp.float32), want)
    out_of = col >= NY * RES

    def below(cands):
        counts = [jnp.zeros((8, 128), jnp.float32) for _ in cands]
        for n in range(NZ * NC):
            for r in range(NX):
                v = jnp.broadcast_to(rows2[n, pl.ds(r, 1), :], (8, 128))
                v = jnp.where(out_of, BIG, v)
                counts = [k + jnp.where(v < t, 1.0, 0.0) for k, t in zip(counts, cands)]
        return [jnp.broadcast_to(jnp.sum(k, axis=1, keepdims=True), (8, 128)) for k in counts]

    def pick(lo, cands):
        for k, t in zip(below(cands), cands):
            lo = jnp.where(k <= want, t, lo)
        return lo

    tiny = 2.0**-126
    lo = jnp.full((8, 128), tiny, jnp.float32)
    for e in (64, 16, 4, 1):
        first = lo * 2.0**e
        lo = pick(lo, [first, first * 2.0**e, first * 2.0**e * 2.0**e])
    unit0 = lo

    def refine(_, carry):
        lo, part = carry
        quarter = part * 0.25
        return pick(lo, [lo + quarter, lo + 2.0 * quarter, lo + 3.0 * quarter]), quarter

    lo, part = lax.fori_loop(0, 11, refine, (lo, unit0))
    lo = pick(lo, [lo + part * 0.5])
    none = below([jnp.full((8, 128), tiny, jnp.float32)])[0] > want
    lo = jnp.where(none, 0.0, lo)
    q_out[...] = jnp.sum(jnp.where(col == rowi, lo, 0.0), axis=0, keepdims=True)[:, :8]

    for copy in sends:
        copy.wait_send()


def shards(hidden, proj_weight, targets, counts, ranks):
    f32, bf16, i32 = jnp.float32, jnp.bfloat16, jnp.int32
    dma = pltpu.SemaphoreType.DMA
    hbm = pl.BlockSpec(memory_space=pl.ANY)
    vmem = pl.BlockSpec(memory_space=pltpu.VMEM)
    ce, means, quantiles = pl.pallas_call(
        kernel,
        out_shape=(
            jax.ShapeDtypeStruct((1, ROWS), f32),
            jax.ShapeDtypeStruct((1, RES), f32),
            jax.ShapeDtypeStruct((1, 8), f32),
        ),
        in_specs=[pl.BlockSpec(memory_space=pltpu.SMEM), hbm, hbm, hbm, hbm],
        out_specs=(vmem, vmem, vmem),
        scratch_shapes=[
            pltpu.VMEM((NX, NY, ROWS, KB), bf16),
            pltpu.VMEM((4, KB, WIDE), bf16),
            pltpu.VMEM((NX, TILES, ROWS, 128), f32),
            pltpu.VMEM((ROWS, 128), f32),
            pltpu.VMEM((ROWS, 128), f32),
            pltpu.VMEM((ROWS, 128), f32),
            pltpu.VMEM((ROWS, 128), f32),
            pltpu.VMEM((NX, ROWS, 128), f32),
            pltpu.VMEM((NX, 1, ROWS), i32),
            pltpu.VMEM((RES, ROWS), i32),
            pltpu.VMEM((32, ROWS), f32),
            pltpu.VMEM((256, ROWS), bf16),
            pltpu.VMEM((NX, 4, ROWS), f32),
            pltpu.VMEM((NX * NY, 4, ROWS), f32),
            pltpu.VMEM((NX * NY, 1, 128), f32),
            pltpu.VMEM((1, 128), f32),
            pltpu.VMEM((NZ * NC, NX, 128), f32),
            pltpu.VMEM((NX, 128), f32),
            dma((2,)),
            dma((4,)), dma((4,)),
            dma((4,)), dma((4,)),
            dma((4, ITEMS)), dma((4, ITEMS)),
            dma((2, ZITEMS)), dma((2, ZITEMS)),
            dma((4 * NZ,)), dma((4 * NZ,)),
            dma((16,)), dma((16,)),
            dma((16,)), dma((16,)),
            dma((16,)), dma((16,)),
        ],
        compiler_params=pltpu.CompilerParams(
            collective_id=0, has_side_effects=True, vmem_limit_bytes=60 * 2**20
        ),
    )(ranks, hidden, proj_weight, targets.reshape(1, ROWS), counts)
    return ce.reshape(ROWS), means, quantiles.reshape(8)


def solution(mesh):
    return jax.shard_map(
        shards,
        mesh=mesh,
        in_specs=(
            P("subset", "vocab"),
            P("subset", "vocab"),
            P("subset"),
            P("subset", "vocab", None),
            P(),
        ),
        out_specs=(P("subset"), P("subset", "vocab"), P()),
        check_vma=False,
    )
```

time: 226 us -> 109 us (0.48)
  waiting for transfers between devices: 127 us -> 0 us
  Pallas kernels: 0 us -> 104 us
  blocking collectives: 24.1 us -> 0 us
  matrix products: 22.3 us -> 0 us
  other arithmetic: 16.5 us -> 0 us
  between operations: 14.2 us -> 0.65 us
  starting transfers between devices: 8.79 us -> 0 us
  local copies, waits for them, and re-layouts: 12.4 us -> 3.92 us
    pallas_call x0 -> x1, Pallas kernels: none -> 104 us  [shards(): pl.pallas_call(kernel, out_shape=(jax.ShapeDtypeStruct((1, ROWS), f32), j...]
    all_gather x1 -> x0, waiting for transfers between devices: 98.7 us -> none  [shards(): whole_weight = lax.all_gather(proj_weight, 'subset', axis=0, tiled=True)]
    all_to_all x2 -> x0, waiting for transfers between devices: 28.1 us -> none  [copy_for_each(): return lax.all_to_all(copies, axis, split_axis=0, concat_axis=0, tiled=True)]
    all_to_all x2 -> x0, blocking collectives: 24.1 us -> none  [copy_for_each(): return lax.all_to_all(copies, axis, split_axis=0, concat_axis=0, tiled=True)]
    dot_general x2 -> x0, matrix products: 22.3 us -> none  [the longest x1 22.2 us: shards(): jnp.dot(features, whole_weight, preferred_element_type=jnp.float32)]
    all_to_all x2 -> x0, starting transfers between devices: 8.76 us -> none  [copy_for_each(): return lax.all_to_all(copies, axis, split_axis=0, concat_axis=0, tiled=True)]
    gather x1 -> x0, local copies, waits for them, and re-layouts: 8.14 us -> none  [shards(): jnp.take_along_axis(logit_scores, jnp.clip(offset, 0, columns - 1)[:, Non...]
    reduce_sum x2 -> x0, other arithmetic: 7.36 us -> none  [the longest x1 6.61 us: shards(): local_sum = jnp.sum(jnp.exp(logit_scores - local_top[:, None]), axis=1)]
  transfers between devices with their start and end apart: 3 -> 0, of which waited for: 3 -> 0; matrix products, arithmetic and copies ran while one was open for 2% -> 0% of each run, Pallas kernels for 0% -> 0%
where the time goes in v1:
time: 109 us
  Pallas kernels  104 us (95%)
  local copies, waits for them, and re-layouts  3.92 us (4%)
    pallas_call x1, Pallas kernels, shards(): pl.pallas_call(kernel, out_shape=(jax.ShapeDtypeStruct((1, ROWS), f32), j...  104 us
    unnamed x10, local copies, waits for them, and re-layouts  3.92 us

profile of v1, /device:TPU:1, one launch (start us, length us, event | category | flops | bytes accessed | tf_op | source)
XLA Modules:
  0.0 108.6 jit_solution(16885141902302708605)
XLA Ops:
  0.6 1.4 %copy.8.c_in = s32[1,25,512]{2,1,0:T(8,128)} copy(s32[1,25,512]{2,0,1:T(1,128)} %param.8) | data formatting | bytes 102400 | tf_op args[3]
  2.1 104.1 %shard_map.76 = (f32[1,512]{1,0:T(1,128)}, f32[1,25]{1,0:T(1,128)}, f32[1,8]{1,0:T(1,128)}) custom-call(s32[8]{0:T(128)} %ranks.1, bf16[512,512]{1,0:T(8,128)(2,1)} %h_in.1, bf16[32,6400]{1,0:T(8,128)(2,1)} %w_in.1, s32[1,512]{1,0:T(1,128)} %bitcast.3, s32[1,25,512]{2,1,0:T(8,128)} %copy.8.c_in), custom_call_target="tpu_custom_call" | custom-call | tf_op jit(solution)/shard_map/pallas_call | solution.py:452
  106.1 0.0 copy-start
  106.2 0.7 copy-done
  106.8 0.0 copy-start.2
  106.8 0.6 copy.12
  107.4 0.1 copy-done.2
  107.5 0.0 copy-start.1
  107.5 0.5 copy.13
  108.0 0.1 copy-done.1
  108.1 0.5 copy.14
Async XLA Ops:
  106.1 0.7 copy-start
  106.8 0.7 copy-start.2
  107.5 0.7 copy-start.1

commit v2 on v1

v2 whole, which is shorter than its diff:
```python
import jax
import jax.numpy as jnp
from jax import lax
from jax.experimental import pallas as pl
from jax.experimental.pallas import tpu as pltpu
from jax.sharding import PartitionSpec as P

MESH = pl.DeviceIdType.MESH
NX, NY, NZ, NC = 4, 4, 8, 2
ROWS = 512
HALF = 256
QTR = 128
KB = 512
COLS = 6400
TILES = 13
WIDE = TILES * 128
STRIP = 16
RES = 25
ITEMS = 10
ZITEMS = 28
BIG = 3.0e38


def kernel(
    ranks, h_in, w_in, t_in, c_in,
    ce_out, mean_out, q_out,
    hb, wb, acc, apack, tsub, tbuf, cbuf, cpad, call, sbuf, stats_x, joined, stats_y, rows1, mine1, rows2, mine2,
    local_sem, xa_send, xa_recv, t_send, t_recv, h_send, h_recv, z_send, z_recv, c_send, c_recv,
    n_send, n_recv, s_send, s_recv, y_send, y_recv, g_send, g_recv, k_send, k_recv,
):
    sub = lax.axis_index("subset")
    y = lax.axis_index("vocab")
    x = sub // (NZ * NC)
    z = (sub // NC) % NZ
    c = sub % NC

    def at(xx, yy, zz, cc):
        return (((xx + NX) % NX) * (NZ * NC) + ((zz + NZ) % NZ) * NC + (cc + NC) % NC, (yy + NY) % NY)

    def remote(src, dst, ss, rs, dev):
        return pltpu.make_async_remote_copy(
            src_ref=src, dst_ref=dst, send_sem=ss, recv_sem=rs, device_id=dev, device_id_type=MESH
        )

    def local(src, dst, sem):
        return pltpu.make_async_copy(src, dst, sem)

    sends = []

    def start(copy):
        copy.start()
        sends.append(copy)

    def drain():
        for copy in sends:
            copy.wait_send()
        sends.clear()

    barrier = pltpu.get_barrier_semaphore()
    friends = [
        at(x + 1, y, z, c), at(x + 2, y, z, c), at(x + 3, y, z, c), at(x, y + 1, z, c), at(x, y + 3, z, c),
        at(x, y, z + 1, c), at(x, y, z - 1, c), at(x, y, z, c + 1),
    ]
    for friend in friends:
        pl.semaphore_signal(barrier, inc=1, device_id=friend, device_id_type=MESH)

    def colrange(xx):
        return pl.ds(pl.multiple_of(((25 * xx) // 2) * 128, 128), WIDE)

    def strip(zz, cc, half):
        start_row = zz * (NC * 2 * STRIP) + cc * (2 * STRIP)
        if half is None:
            return pl.ds(pl.multiple_of(start_row, 2 * STRIP), 2 * STRIP)
        return pl.ds(pl.multiple_of(start_row + half * STRIP, STRIP), STRIP)

    own_w = local(w_in.at[:, colrange(x)], wb.at[x, strip(z, c, None), :], xa_recv.at[0])
    own_w.start()
    own_h = local(h_in, hb.at[x, y], local_sem.at[0])
    own_h.start()
    own_t = local(t_in, tbuf.at[x], t_recv.at[0])
    own_t.start()
    own_c = local(c_in, cbuf, local_sem.at[1])
    own_c.start()
    pl.semaphore_wait(barrier, len(friends))

    for d in (1, 3, 2):
        xx = (x + d) % NX
        start(
            remote(
                w_in.at[:, colrange(xx)], wb.at[x, strip(z, c, None), :],
                xa_send.at[d], xa_recv.at[(NX - d) % NX], at(xx, y, z, c),
            )
        )

    def wait_cols(q):
        off = (q - x + NX) % NX
        local(w_in.at[:, colrange(0)], wb.at[q, strip(z, c, None), :], xa_recv.at[off]).wait()

    def span(path, part):
        if part is None:
            return pl.ds(path * HALF, HALF)
        return pl.ds(path * HALF + part * QTR, QTR)

    def place(axis, along, cross, path, part):
        along, cross = (along + 4) % 4, (cross + 4) % 4
        xx, yy = (along, cross) if axis == 0 else (cross, along)
        return hb.at[xx, yy, span(path, part), :]

    def item(axis, d, j, me_along, cross):
        first, second = (0, 1) if axis == 0 else (1, 0)
        part = 0 if d == 1 else 1
        back = me_along - d
        if j == 0:
            return place(axis, me_along, cross, first, None)
        if j == 2:
            return place(axis, back, cross, first, part)
        if j in (1, 3, 5, 7):
            return place(axis, me_along, cross + {1: 0, 3: 1, 5: -1, 7: 2}[j], second, None)
        return place(axis, back, cross + {4: 0, 6: 1, 8: -1, 9: 2}[j], second, part)

    def links():
        for axis in (0, 1):
            for d in (1, -1):
                yield axis, d, 2 * axis + (0 if d == 1 else 1)

    def coords(axis):
        return (x, y) if axis == 0 else (y, x)

    def neighbour(axis, d):
        return at(x + d, y, z, c) if axis == 0 else at(x, y + d, z, c)

    def send_h(j):
        for axis, d, n in links():
            along, cross = coords(axis)
            dst = item(axis, d, j, along, cross)
            first, second = (0, 1) if axis == 0 else (1, 0)
            src = dst
            if j == 0:
                src = h_in.at[span(first, None), :]
            if j == 1:
                src = h_in.at[span(second, None), :]
            start(remote(src, dst, h_send.at[n, j], h_recv.at[n, j], neighbour(axis, d)))

    def wait_h(j):
        for axis, d, n in links():
            along, cross = coords(axis)
            got = item(axis, d, j, along - d, cross)
            remote(got, got, h_send.at[n, j], h_recv.at[n, j], neighbour(axis, d)).wait_recv()

    send_h(0)
    send_h(1)

    for d in (1, 2, 3):
        start(
            remote(t_in, tbuf.at[x], t_send.at[d], t_recv.at[(NX - d) % NX], at(x + d, y, z, c))
        )

    order = [y, (y + 1) % 4, (y + 3) % 4, (y + 2) % 4]

    def zitem(d, j):
        quarter, i = divmod(j, 7)
        turn = 0 if d == 1 else 1
        return quarter, (i + turn) % 2, i // 2

    def send_core(o, hops):
        ref = wb.at[order[o], strip((z - hops + NZ) % NZ, c, None), :]
        n = o * NZ + hops % NZ
        start(remote(ref, ref, c_send.at[n], c_recv.at[n], at(x, y, z, c + 1)))

    def wait_core(o):
        for hops in range(NZ):
            ref = wb.at[order[o], strip((z - hops + NZ) % NZ, (c + 1) % NC, None), :]
            n = o * NZ + hops
            remote(ref, ref, c_send.at[n], c_recv.at[n], at(x, y, z, c + 1)).wait_recv()

    def send_z(j):
        for i, d in enumerate((1, -1)):
            o, half, k = zitem(d, j)
            ref = wb.at[order[o], strip((z - d * k + NZ) % NZ, c, half), :]
            start(remote(ref, ref, z_send.at[i, j], z_recv.at[i, j], at(x, y, z + d, c)))

    def own_cols(o):
        wait_cols(order[o])
        send_core(o, 0)

    def step_z(j):
        for i, d in enumerate((1, -1)):
            o, half, k = zitem(d, j)
            ref = wb.at[order[o], strip((z - d * (k + 1) + NZ) % NZ, c, half), :]
            remote(ref, ref, z_send.at[i, j], z_recv.at[i, j], at(x, y, z + d, c)).wait_recv()
        if j + 2 < ZITEMS:
            if (j + 2) % 7 == 0:
                own_cols((j + 2) // 7)
            send_z(j + 2)
        if j % 7 in (1, 3, 5):
            for d in (1, -1):
                o, half, k = zitem(d, j)
                send_core(o, d * (k + 1))
        if j % 7 == 6:
            send_core(j // 7, 4)

    own_cols(0)
    send_z(0)
    send_z(1)

    odd = (x % 2).astype(jnp.float32)
    keep = 1.0 - odd
    away = odd * 1048576.0
    base = (y * COLS + ((25 * x) // 2) * 128).astype(jnp.float32)

    def prepare():
        own_c.wait()
        cpad[...] = jnp.zeros(cpad.shape, jnp.float32)
        for i in range(RES):
            cpad[pl.ds(i, 1), :] = cbuf[i].astype(jnp.float32)
        call[y] = cpad[...].astype(jnp.bfloat16)
        for d in (1, 3, 2):
            ref = call.at[y]
            start(remote(ref, ref, n_send.at[d], n_recv.at[(NY - d) % NY], at(x, y + d, z, c)))
        own_t.wait()
        for d in (1, 2, 3):
            ref = tbuf.at[(x + d) % NX]
            remote(ref, ref, t_send.at[d], t_recv.at[d], at(x + d, y, z, c)).wait_recv()
        lane = lax.broadcasted_iota(jnp.int32, (ROWS, 128), 1).astype(jnp.float32)
        for b in range(NX):
            t = tbuf[b].astype(jnp.float32) - base
            tsub[b] = jnp.broadcast_to(t, (128, ROWS)).T - lane
        apack[...] = jnp.zeros(apack.shape, jnp.float32)

    def block(dx):
        return (x + dx) % NX

    def unit(dx, o):
        b, q = block(dx), order[o]
        part = jnp.dot(hb[b, q], wb[q], preferred_element_type=jnp.float32)
        if o == 0:
            acc[b] = part
        else:
            acc[b] += part

    def finish(dx):
        b = block(dx)

        @pl.loop(0, ROWS // 64)
        def _(r):
            rows = pl.ds(pl.multiple_of(r * 64, 64), 64)

            def piece(j):
                return acc[b, rows, pl.ds(j * 128, 128)]

            top = piece(0)
            for j in range(1, TILES):
                top = jnp.maximum(top, piece(j))
            top = jnp.broadcast_to(jnp.max(top, axis=1, keepdims=True), (64, 128))
            want = tsub[b, rows, :]
            total = jnp.exp(piece(0) - top) * keep
            picked = jnp.where(want + away == 0.0, piece(0), 0.0)
            for j in range(1, TILES):
                value = piece(j)
                total = total + jnp.exp(value - top)
                picked = jnp.where(want == j * 128.0, value, picked)
            total = jnp.sum(total, axis=1, keepdims=True)
            picked = jnp.sum(picked, axis=1, keepdims=True)
            lane = lax.broadcasted_iota(jnp.int32, (64, 128), 1)
            group = r // 2
            to = pl.ds(pl.multiple_of((r % 2) * 64, 64), 64)
            apack[to, :] = jnp.where(
                lane == group, top, jnp.where(lane == group + 4, total, jnp.where(lane == group + 8, picked, apack[to, :]))
            )

        sbuf[b] = apack[...].T[:16]
        if dx:
            m = NX - dx
            start(remote(sbuf.at[b], stats_x.at[m], s_send.at[dx], s_recv.at[m], at(b, y, z, c)))

    wait_h(0)
    send_h(2)
    send_h(3)
    step_z(0)
    step_z(1)
    prepare()
    for j in (2, 3, 4):
        step_z(j)
    wait_h(1)
    send_h(4)
    step_z(5)
    step_z(6)
    own_h.wait()
    wait_core(0)
    unit(0, 0)
    step_z(7)
    wait_h(2)
    send_h(5)
    unit(1, 0)
    step_z(8)
    unit(3, 0)
    for j in (9, 10, 11):
        step_z(j)
    wait_h(3)
    send_h(6)
    step_z(12)
    step_z(13)
    wait_core(1)
    unit(0, 1)
    step_z(14)
    wait_h(4)
    send_h(7)
    unit(1, 1)
    step_z(15)
    unit(2, 0)
    for j in (16, 17, 18):
        step_z(j)
    wait_h(5)
    send_h(8)
    step_z(19)
    step_z(20)
    unit(3, 1)
    step_z(21)
    wait_core(2)
    unit(0, 2)
    wait_h(6)
    step_z(22)
    unit(1, 2)
    step_z(23)
    unit(3, 2)
    step_z(24)
    step_z(25)
    wait_h(7)
    send_h(9)
    unit(2, 1)
    step_z(26)
    step_z(27)
    wait_core(3)
    unit(0, 3)
    finish(0)
    unit(1, 3)
    finish(1)
    wait_h(8)
    unit(2, 2)
    unit(3, 3)
    finish(3)
    wait_h(9)
    unit(2, 3)
    finish(2)

    drain()
    for d in (1, 2, 3):
        ref = call.at[(y + d) % NY]
        remote(ref, ref, n_send.at[d], n_recv.at[d], at(x, y + d, z, c)).wait_recv()

    def join(parts):
        tops = [p[0:4] for p in parts]
        top = jnp.maximum(jnp.maximum(tops[0], tops[1]), jnp.maximum(tops[2], tops[3]))
        total = parts[0][4:8] * jnp.exp(tops[0] - top)
        target = parts[0][8:12]
        for p, t in zip(parts[1:], tops[1:]):
            total = total + p[4:8] * jnp.exp(t - top)
            target = target + p[8:12]
        return top, total, target

    for d in (1, 3, 2):
        ref = stats_x.at[d]
        remote(ref, ref, s_send.at[d], s_recv.at[d], at(x + d, y, z, c)).wait_recv()
    top, total, target = join([sbuf[x], stats_x[1], stats_x[2], stats_x[3]])
    joined[pl.ds(0, 4), :] = top
    joined[pl.ds(4, 4), :] = total
    joined[pl.ds(8, 4), :] = target
    joined[pl.ds(12, 4), :] = target
    for d in (2, 1, 3):
        m = NY - d
        start(remote(joined, stats_y.at[m], y_send.at[d], y_recv.at[m], at(x, y + d, z, c)))
    for d in (1, 3, 2):
        ref = stats_y.at[d]
        remote(ref, ref, y_send.at[d], y_recv.at[d], at(x, y + d, z, c)).wait_recv()
    top, total, target = join([joined[...], stats_y[1], stats_y[2], stats_y[3]])
    ce = top + jnp.log(total) - target
    ce_out[...] = ce

    ce = jnp.concatenate([ce[g : g + 1] for g in range(4)], axis=1)
    high = ce.astype(jnp.bfloat16).astype(jnp.float32)
    middle = (ce - high).astype(jnp.bfloat16).astype(jnp.float32)
    low = (ce - high) - middle
    which = lax.broadcasted_iota(jnp.int32, (16, ROWS), 0)
    pieces = jnp.where(which == 0, high, jnp.where(which == 1, middle, jnp.where(which == 2, low, 0.0)))
    pieces = pieces.astype(jnp.bfloat16)

    def means_of(rhs):
        sums = lax.dot_general(
            pieces, rhs, (((1,), (1,)), ((), ())), preferred_element_type=jnp.float32
        )
        return jnp.sum(sums, axis=0, keepdims=True) * (1.0 / 32768.0)

    means = means_of(call[...].reshape(128, ROWS))
    lanes = lax.broadcasted_iota(jnp.int32, (1, 128), 1)
    mine1[...] = jnp.where(lanes % 32 < RES, means, BIG)

    others = [(dx, dc) for dx in range(NX) for dc in range(NC) if (dx, dc) != (0, 0)]
    for dx, dc in others:
        n, m = dx * NC + dc, ((NX - dx) % NX) * NC + dc
        start(remote(mine1, rows1.at[m], g_send.at[n], g_recv.at[m], at(x + dx, y, z, c + dc)))
    mean_out[...] = means_of(call[y])[:, :RES]
    mine2[pl.ds(0, 1), :] = mine1[...]
    for dx, dc in others:
        n = dx * NC + dc
        ref = rows1.at[n]
        remote(ref, ref, g_send.at[n], g_recv.at[n], at(x + dx, y, z, c + dc)).wait_recv()
        mine2[pl.ds(n, 1), :] = rows1[n]
    for d in (4, 3, 5, 2, 6, 1, 7):
        m = NZ - d
        start(remote(mine2, rows2.at[m], k_send.at[d], k_recv.at[m], at(x, y, z + d, c)))
    rows2[0] = mine2[...]
    for d in (1, 7, 2, 6, 3, 5, 4):
        ref = rows2.at[d]
        remote(ref, ref, k_send.at[d], k_recv.at[d], at(x, y, z + d, c)).wait_recv()

    col = lax.broadcasted_iota(jnp.int32, (8, 128), 1)
    rowi = lax.broadcasted_iota(jnp.int32, (8, 128), 0)
    want = jnp.zeros((8, 128), jnp.float32)
    for q in range(8):
        want = jnp.where(rowi == q, ranks[q].astype(jnp.float32), want)

    def below(cands):
        counts = [jnp.zeros((8, 128), jnp.float32) for _ in cands]
        for n in range(NZ):
            for r in range(8):
                v = jnp.broadcast_to(rows2[n, pl.ds(r, 1), :], (8, 128))
                counts = [k + jnp.where(v < t, 1.0, 0.0) for k, t in zip(counts, cands)]
        return [jnp.broadcast_to(jnp.sum(k, axis=1, keepdims=True), (8, 128)) for k in counts]

    def pick(lo, cands):
        for k, t in zip(below(cands), cands):
            lo = jnp.where(k <= want, t, lo)
        return lo

    tiny = 2.0**-126
    lo = jnp.full((8, 128), tiny, jnp.float32)
    for e in (64, 16, 4, 1):
        first = lo * 2.0**e
        lo = pick(lo, [first, first * 2.0**e, first * 2.0**e * 2.0**e])
    unit0 = lo

    def refine(_, carry):
        lo, part = carry
        quarter = part * 0.25
        return pick(lo, [lo + quarter, lo + 2.0 * quarter, lo + 3.0 * quarter]), quarter

    lo, part = lax.fori_loop(0, 11, refine, (lo, unit0))
    lo = pick(lo, [lo + part * 0.5])
    none = below([jnp.full((8, 128), tiny, jnp.float32)])[0] > want
    lo = jnp.where(none, 0.0, lo)
    q_out[...] = jnp.sum(jnp.where(col == rowi, lo, 0.0), axis=0, keepdims=True)[:, :8]
    drain()


def shards(hidden, proj_weight, targets, counts, ranks):
    f32, bf16, i32 = jnp.float32, jnp.bfloat16, jnp.int32
    dma = pltpu.SemaphoreType.DMA
    hbm = pl.BlockSpec(memory_space=pl.ANY)
    vmem = pl.BlockSpec(memory_space=pltpu.VMEM)
    ce, means, quantiles = pl.pallas_call(
        kernel,
        out_shape=(
            jax.ShapeDtypeStruct((4, 128), f32),
            jax.ShapeDtypeStruct((1, RES), f32),
            jax.ShapeDtypeStruct((1, 8), f32),
        ),
        in_specs=[pl.BlockSpec(memory_space=pltpu.SMEM), hbm, hbm, hbm, hbm],
        out_specs=(vmem, vmem, vmem),
        scratch_shapes=[
            pltpu.VMEM((NX, NY, ROWS, KB), bf16),
            pltpu.VMEM((4, KB, WIDE), bf16),
            pltpu.VMEM((NX, ROWS, WIDE), f32),
            pltpu.VMEM((128, 128), f32),
            pltpu.VMEM((NX, ROWS, 128), f32),
            pltpu.VMEM((NX, 1, ROWS), i32),
            pltpu.VMEM((RES, 1, ROWS), i32),
            pltpu.VMEM((32, ROWS), f32),
            pltpu.VMEM((NY, 32, ROWS), bf16),
            pltpu.VMEM((NX, 16, 128), f32),
            pltpu.VMEM((NX, 16, 128), f32),
            pltpu.VMEM((16, 128), f32),
            pltpu.VMEM((NY, 16, 128), f32),
            pltpu.VMEM((8, 1, 128), f32),
            pltpu.VMEM((1, 128), f32),
            pltpu.VMEM((NZ, 8, 128), f32),
            pltpu.VMEM((8, 128), f32),
            dma((2,)),
            dma((4,)), dma((4,)),
            dma((4,)), dma((4,)),
            dma((4, ITEMS)), dma((4, ITEMS)),
            dma((2, ZITEMS)), dma((2, ZITEMS)),
            dma((4 * NZ,)), dma((4 * NZ,)),
            dma((4,)), dma((4,)),
            dma((4,)), dma((4,)),
            dma((4,)), dma((4,)),
            dma((8,)), dma((8,)),
            dma((8,)), dma((8,)),
        ],
        compiler_params=pltpu.CompilerParams(
            collective_id=0, has_side_effects=True, vmem_limit_bytes=60 * 2**20
        ),
    )(ranks, hidden, proj_weight, targets.reshape(1, ROWS), counts.transpose(1, 0, 2))
    return ce.reshape(ROWS), means, quantiles.reshape(8)


def solution(mesh):
    return jax.shard_map(
        shards,
        mesh=mesh,
        in_specs=(
            P("subset", "vocab"),
            P("subset", "vocab"),
            P("subset"),
            P("subset", "vocab", None),
            P(),
        ),
        out_specs=(P("subset"), P("subset", "vocab"), P()),
        check_vma=False,
    )
```

time: 109 us -> 115 us (1.055)
  Pallas kernels: 104 us -> 112 us
  local copies, waits for them, and re-layouts: 3.92 us -> 2.36 us
    pallas_call x1, Pallas kernels: 104 us -> 112 us  [shards(): pl.pallas_call(kernel, out_shape=(jax.ShapeDtypeStruct((4, 128), f32), ja...]
    unnamed x10 -> x9, local copies, waits for them, and re-layouts: 3.92 us -> 2.36 us
where the time goes in v2:
time: 115 us
  Pallas kernels  112 us (97%)
  local copies, waits for them, and re-layouts  2.36 us (2%)
    pallas_call x1, Pallas kernels, shards(): pl.pallas_call(kernel, out_shape=(jax.ShapeDtypeStruct((4, 128), f32), ja...  112 us
    unnamed x9, local copies, waits for them, and re-layouts  2.36 us

profile of v2, /device:TPU:1, one launch (start us, length us, event | category | flops | bytes accessed | tf_op | source)
XLA Modules:
  0.0 114.9 jit_solution(12433939430967201449)
XLA Ops:
  0.6 111.9 %shard_map.76 = (f32[4,128]{1,0:T(4,128)}, f32[1,25]{1,0:T(1,128)}, f32[1,8]{1,0:T(1,128)}) custom-call(s32[8]{0:T(128)} %ranks.1, bf16[512,512]{1,0:T(8,128)(2,1)} %h_in.1, bf16[32,6400]{1,0:T(8,128)(2,1)} %w_in.1, s32[1,512]{1,0:T(1,128)} %bitcast.5, s32[25,1,512]{2,1,0:T(1,128)} %bitcast.4), custom_call_target="tpu_custom_call" | custom-call | tf_op jit(solution)/shard_map/pallas_call | solution.py:460
  112.6 0.0 copy-start
  112.6 0.6 copy-done
  113.2 0.0 copy-start.2
  113.2 0.6 copy.11
  113.8 0.0 copy-done.2
  113.8 0.0 copy-start.1
  113.8 0.5 copy.12
  114.3 0.1 copy-done.1
  114.4 0.5 copy.13
Async XLA Ops:
  112.6 0.7 copy-start
  113.2 0.6 copy-start.2
  113.8 0.6 copy-start.1

commit v3 on v2

--- a/solution.py
+++ b/solution.py
@@ -8,25 +8,27 @@
 MESH = pl.DeviceIdType.MESH
 NX, NY, NZ, NC = 4, 4, 8, 2
 ROWS = 512
-HALF = 256
-QTR = 128
+SHARES = {
+    (0, None): (0, 272), (0, 0): (0, 144), (0, 1): (144, 128),
+    (1, None): (272, 240), (1, 0): (272, 128), (1, 1): (400, 112),
+}
 KB = 512
 COLS = 6400
 TILES = 13
 WIDE = TILES * 128
-STRIP = 16
+STRIP = 32
 RES = 25
 ITEMS = 10
-ZITEMS = 28
+ZITEMS = 14
 BIG = 3.0e38
 
 
 def kernel(
     ranks, h_in, w_in, t_in, c_in,
     ce_out, mean_out, q_out,
-    hb, wb, acc, apack, tsub, tbuf, cbuf, cpad, call, sbuf, stats_x, joined, stats_y, rows1, mine1, rows2, mine2,
+    hb, wb, acc, tsub, tbuf, cbuf, cpad, call, sbuf, stats, rows1, mine1, rows2, mine2,
     local_sem, xa_send, xa_recv, t_send, t_recv, h_send, h_recv, z_send, z_recv, c_send, c_recv,
-    n_send, n_recv, s_send, s_recv, y_send, y_recv, g_send, g_recv, k_send, k_recv,
+    n_send, n_recv, s_send, s_recv, g_send, g_recv, k_send, k_recv,
 ):
     sub = lax.axis_index("subset")
     y = lax.axis_index("vocab")
@@ -67,13 +69,10 @@
     def colrange(xx):
         return pl.ds(pl.multiple_of(((25 * xx) // 2) * 128, 128), WIDE)
 
-    def strip(zz, cc, half):
-        start_row = zz * (NC * 2 * STRIP) + cc * (2 * STRIP)
-        if half is None:
-            return pl.ds(pl.multiple_of(start_row, 2 * STRIP), 2 * STRIP)
-        return pl.ds(pl.multiple_of(start_row + half * STRIP, STRIP), STRIP)
-
-    own_w = local(w_in.at[:, colrange(x)], wb.at[x, strip(z, c, None), :], xa_recv.at[0])
+    def strip(zz, cc):
+        return pl.ds(pl.multiple_of(zz * (NC * STRIP) + cc * STRIP, STRIP), STRIP)
+
+    own_w = local(w_in.at[:, colrange(x)], wb.at[x, strip(z, c), :], xa_recv.at[0])
     own_w.start()
     own_h = local(h_in, hb.at[x, y], local_sem.at[0])
     own_h.start()
@@ -87,19 +86,18 @@
         xx = (x + d) % NX
         start(
             remote(
-                w_in.at[:, colrange(xx)], wb.at[x, strip(z, c, None), :],
+                w_in.at[:, colrange(xx)], wb.at[x, strip(z, c), :],
                 xa_send.at[d], xa_recv.at[(NX - d) % NX], at(xx, y, z, c),
             )
         )
 
     def wait_cols(q):
         off = (q - x + NX) % NX
-        local(w_in.at[:, colrange(0)], wb.at[q, strip(z, c, None), :], xa_recv.at[off]).wait()
+        local(w_in.at[:, colrange(0)], wb.at[q, strip(z, c), :], xa_recv.at[off]).wait()
 
     def span(path, part):
-        if part is None:
-            return pl.ds(path * HALF, HALF)
-        return pl.ds(path * HALF + part * QTR, QTR)
+        first, count = SHARES[path, part]
+        return pl.ds(first, count)
 
     def place(axis, along, cross, path, part):
         along, cross = (along + 4) % 4, (cross + 4) % 4
@@ -155,29 +153,30 @@
             remote(t_in, tbuf.at[x], t_send.at[d], t_recv.at[(NX - d) % NX], at(x + d, y, z, c))
         )
 
-    order = [y, (y + 1) % 4, (y + 3) % 4, (y + 2) % 4]
+    far = ((y - x + 4) % 4) // 2
+    order = [(y + far) % 4, (y + 1 - far) % 4, (y + 3) % 4, (y + 2) % 4]
 
     def zitem(d, j):
-        quarter, i = divmod(j, 7)
+        pair, i = divmod(j, 7)
         turn = 0 if d == 1 else 1
-        return quarter, (i + turn) % 2, i // 2
+        return 2 * pair + (i + turn) % 2, i // 2
 
     def send_core(o, hops):
-        ref = wb.at[order[o], strip((z - hops + NZ) % NZ, c, None), :]
+        ref = wb.at[order[o], strip((z - hops + NZ) % NZ, c), :]
         n = o * NZ + hops % NZ
         start(remote(ref, ref, c_send.at[n], c_recv.at[n], at(x, y, z, c + 1)))
 
     def wait_core(o):
         for hops in range(NZ):
-            ref = wb.at[order[o], strip((z - hops + NZ) % NZ, (c + 1) % NC, None), :]
+            ref = wb.at[order[o], strip((z - hops + NZ) % NZ, (c + 1) % NC), :]
             n = o * NZ + hops
             remote(ref, ref, c_send.at[n], c_recv.at[n], at(x, y, z, c + 1)).wait_recv()
 
-    def send_z(j):
-        for i, d in enumerate((1, -1)):
-            o, half, k = zitem(d, j)
-            ref = wb.at[order[o], strip((z - d * k + NZ) % NZ, c, half), :]
-            start(remote(ref, ref, z_send.at[i, j], z_recv.at[i, j], at(x, y, z + d, c)))
+    def send_z(j, d):
+        o, k = zitem(d, j)
+        i = 0 if d == 1 else 1
+        ref = wb.at[order[o], strip((z - d * k + NZ) % NZ, c), :]
+        start(remote(ref, ref, z_send.at[i, j], z_recv.at[i, j], at(x, y, z + d, c)))
 
     def own_cols(o):
         wait_cols(order[o])
@@ -185,23 +184,24 @@
 
     def step_z(j):
         for i, d in enumerate((1, -1)):
-            o, half, k = zitem(d, j)
-            ref = wb.at[order[o], strip((z - d * (k + 1) + NZ) % NZ, c, half), :]
+            o, k = zitem(d, j)
+            ref = wb.at[order[o], strip((z - d * (k + 1) + NZ) % NZ, c), :]
             remote(ref, ref, z_send.at[i, j], z_recv.at[i, j], at(x, y, z + d, c)).wait_recv()
-        if j + 2 < ZITEMS:
-            if (j + 2) % 7 == 0:
-                own_cols((j + 2) // 7)
-            send_z(j + 2)
-        if j % 7 in (1, 3, 5):
-            for d in (1, -1):
-                o, half, k = zitem(d, j)
-                send_core(o, d * (k + 1))
-        if j % 7 == 6:
-            send_core(j // 7, 4)
+            if j + 2 == 7 and d == 1:
+                own_cols(2)
+                own_cols(3)
+            if j + 2 < ZITEMS:
+                send_z(j + 2, d)
+        for d in (1, -1):
+            o, k = zitem(d, j)
+            send_core(o, d * (k + 1))
 
     own_cols(0)
-    send_z(0)
-    send_z(1)
+    send_z(0, 1)
+    send_z(1, -1)
+    own_cols(1)
+    send_z(0, -1)
+    send_z(1, 1)
 
     odd = (x % 2).astype(jnp.float32)
     keep = 1.0 - odd
@@ -225,15 +225,15 @@
         for b in range(NX):
             t = tbuf[b].astype(jnp.float32) - base
             tsub[b] = jnp.broadcast_to(t, (128, ROWS)).T - lane
-        apack[...] = jnp.zeros(apack.shape, jnp.float32)
 
     def block(dx):
         return (x + dx) % NX
 
-    def unit(dx, o):
-        b, q = block(dx), order[o]
-        part = jnp.dot(hb[b, q], wb[q], preferred_element_type=jnp.float32)
-        if o == 0:
+    def unit(dx, pair):
+        b, ka, kb = block(dx), order[2 * pair], order[2 * pair + 1]
+        part = jnp.dot(hb[b, ka], wb[ka], preferred_element_type=jnp.float32)
+        part = part + jnp.dot(hb[b, kb], wb[kb], preferred_element_type=jnp.float32)
+        if pair == 0:
             acc[b] = part
         else:
             acc[b] += part
@@ -241,138 +241,108 @@
     def finish(dx):
         b = block(dx)
 
-        @pl.loop(0, ROWS // 64)
-        def _(r):
-            rows = pl.ds(pl.multiple_of(r * 64, 64), 64)
-
-            def piece(j):
-                return acc[b, rows, pl.ds(j * 128, 128)]
-
-            top = piece(0)
-            for j in range(1, TILES):
-                top = jnp.maximum(top, piece(j))
-            top = jnp.broadcast_to(jnp.max(top, axis=1, keepdims=True), (64, 128))
-            want = tsub[b, rows, :]
-            total = jnp.exp(piece(0) - top) * keep
-            picked = jnp.where(want + away == 0.0, piece(0), 0.0)
-            for j in range(1, TILES):
-                value = piece(j)
-                total = total + jnp.exp(value - top)
-                picked = jnp.where(want == j * 128.0, value, picked)
-            total = jnp.sum(total, axis=1, keepdims=True)
-            picked = jnp.sum(picked, axis=1, keepdims=True)
-            lane = lax.broadcasted_iota(jnp.int32, (64, 128), 1)
-            group = r // 2
-            to = pl.ds(pl.multiple_of((r % 2) * 64, 64), 64)
-            apack[to, :] = jnp.where(
-                lane == group, top, jnp.where(lane == group + 4, total, jnp.where(lane == group + 8, picked, apack[to, :]))
-            )
-
-        sbuf[b] = apack[...].T[:16]
-        if dx:
-            m = NX - dx
-            start(remote(sbuf.at[b], stats_x.at[m], s_send.at[dx], s_recv.at[m], at(b, y, z, c)))
+        lane = lax.broadcasted_iota(jnp.int32, (64, 128), 1)
+        halves = []
+        for half in range(2):
+            packed = jnp.zeros((64, 128), jnp.float32)
+            for group in range(4):
+                rows = pl.ds(group * 128 + half * 64, 64)
+
+                def piece(j):
+                    return acc[b, rows, pl.ds(j * 128, 128)]
+
+                top = piece(0)
+                for j in range(1, TILES):
+                    top = jnp.maximum(top, piece(j))
+                top = jnp.broadcast_to(jnp.max(top, axis=1, keepdims=True), (64, 128))
+                want = tsub[b, rows, :]
+                total = jnp.exp(piece(0) - top) * keep
+                picked = jnp.where(want + away == 0.0, piece(0), 0.0)
+                for j in range(1, TILES):
+                    value = piece(j)
+                    total = total + jnp.exp(value - top)
+                    picked = jnp.where(want == j * 128.0, value, picked)
+                total = jnp.sum(total, axis=1, keepdims=True)
+                picked = jnp.sum(picked, axis=1, keepdims=True)
+                for k, value in enumerate((top, total, picked)):
+                    packed = jnp.where(lane == group + 4 * k, value, packed)
+            halves.append(packed)
+        sbuf[b] = jnp.concatenate(halves, axis=0).T[:16]
+        for dy in (2, 1, 3, 0):
+            n = dx * NY + dy
+            m = ((NX - dx) % NX) * NY + (NY - dy) % NY
+            if n:
+                start(remote(sbuf.at[b], stats.at[m], s_send.at[n], s_recv.at[m], at(b, y + dy, z, c)))
 
     wait_h(0)
     send_h(2)
     send_h(3)
     step_z(0)
     step_z(1)
-    prepare()
-    for j in (2, 3, 4):
-        step_z(j)
+    step_z(2)
     wait_h(1)
     send_h(4)
+    step_z(3)
+    prepare()
+    wait_h(2)
+    send_h(5)
+    step_z(4)
     step_z(5)
     step_z(6)
+    wait_h(3)
+    send_h(6)
     own_h.wait()
     wait_core(0)
-    unit(0, 0)
+    wait_core(1)
     step_z(7)
-    wait_h(2)
-    send_h(5)
-    unit(1, 0)
-    step_z(8)
-    unit(3, 0)
-    for j in (9, 10, 11):
-        step_z(j)
-    wait_h(3)
-    send_h(6)
-    step_z(12)
-    step_z(13)
-    wait_core(1)
-    unit(0, 1)
-    step_z(14)
     wait_h(4)
     send_h(7)
-    unit(1, 1)
-    step_z(15)
-    unit(2, 0)
-    for j in (16, 17, 18):
-        step_z(j)
+    step_z(8)
+    unit(0, 0)
+    step_z(9)
     wait_h(5)
     send_h(8)
-    step_z(19)
-    step_z(20)
-    unit(3, 1)
-    step_z(21)
-    wait_core(2)
-    unit(0, 2)
+    step_z(10)
+    unit(1, 0)
     wait_h(6)
-    step_z(22)
-    unit(1, 2)
-    step_z(23)
-    unit(3, 2)
-    step_z(24)
-    step_z(25)
+    step_z(11)
+    step_z(12)
     wait_h(7)
     send_h(9)
-    unit(2, 1)
-    step_z(26)
-    step_z(27)
+    step_z(13)
+    unit(3, 0)
+    wait_core(2)
     wait_core(3)
-    unit(0, 3)
+    unit(0, 1)
+    unit(2, 0)
+    wait_h(8)
     finish(0)
-    unit(1, 3)
+    unit(1, 1)
     finish(1)
-    wait_h(8)
-    unit(2, 2)
-    unit(3, 3)
+    unit(3, 1)
     finish(3)
     wait_h(9)
-    unit(2, 3)
+    unit(2, 1)
     finish(2)
 
     drain()
     for d in (1, 2, 3):
         ref = call.at[(y + d) % NY]
         remote(ref, ref, n_send.at[d], n_recv.at[d], at(x, y + d, z, c)).wait_recv()
-
-    def join(parts):
-        tops = [p[0:4] for p in parts]
-        top = jnp.maximum(jnp.maximum(tops[0], tops[1]), jnp.maximum(tops[2], tops[3]))
-        total = parts[0][4:8] * jnp.exp(tops[0] - top)
-        target = parts[0][8:12]
-        for p, t in zip(parts[1:], tops[1:]):
-            total = total + p[4:8] * jnp.exp(t - top)
-            target = target + p[8:12]
-        return top, total, target
-
-    for d in (1, 3, 2):
-        ref = stats_x.at[d]
-        remote(ref, ref, s_send.at[d], s_recv.at[d], at(x + d, y, z, c)).wait_recv()
-    top, total, target = join([sbuf[x], stats_x[1], stats_x[2], stats_x[3]])
-    joined[pl.ds(0, 4), :] = top
-    joined[pl.ds(4, 4), :] = total
-    joined[pl.ds(8, 4), :] = target
-    joined[pl.ds(12, 4), :] = target
-    for d in (2, 1, 3):
-        m = NY - d
-        start(remote(joined, stats_y.at[m], y_send.at[d], y_recv.at[m], at(x, y + d, z, c)))
-    for d in (1, 3, 2):
-        ref = stats_y.at[d]
-        remote(ref, ref, y_send.at[d], y_recv.at[d], at(x, y + d, z, c)).wait_recv()
-    top, total, target = join([joined[...], stats_y[1], stats_y[2], stats_y[3]])
+    for n in range(1, NX * NY):
+        ref = stats.at[n]
+        remote(ref, ref, s_send.at[n], s_recv.at[n], at(x, y, z, c)).wait_recv()
+
+    parts = [sbuf[x]] + [stats[n] for n in range(1, NX * NY)]
+    tops = [p[0:4] for p in parts]
+    top = tops[0]
+    for t in tops[1:]:
+        top = jnp.maximum(top, t)
+    total = jnp.zeros((4, 128), jnp.float32)
+    target = jnp.zeros((4, 128), jnp.float32)
+    for p, t in zip(parts, tops):
+        total = total + p[4:8] * jnp.exp(t - top)
+        target = target + p[8:12]
     ce = top + jnp.log(total) - target
     ce_out[...] = ce
 
@@ -470,16 +440,13 @@
             pltpu.VMEM((NX, NY, ROWS, KB), bf16),
             pltpu.VMEM((4, KB, WIDE), bf16),
             pltpu.VMEM((NX, ROWS, WIDE), f32),
-            pltpu.VMEM((128, 128), f32),
             pltpu.VMEM((NX, ROWS, 128), f32),
             pltpu.VMEM((NX, 1, ROWS), i32),
             pltpu.VMEM((RES, 1, ROWS), i32),
             pltpu.VMEM((32, ROWS), f32),
             pltpu.VMEM((NY, 32, ROWS), bf16),
             pltpu.VMEM((NX, 16, 128), f32),
-            pltpu.VMEM((NX, 16, 128), f32),
-            pltpu.VMEM((16, 128), f32),
-            pltpu.VMEM((NY, 16, 128), f32),
+            pltpu.VMEM((NX * NY, 16, 128), f32),
             pltpu.VMEM((8, 1, 128), f32),
             pltpu.VMEM((1, 128), f32),
             pltpu.VMEM((NZ, 8, 128), f32),
@@ -491,8 +458,7 @@
             dma((2, ZITEMS)), dma((2, ZITEMS)),
             dma((4 * NZ,)), dma((4 * NZ,)),
             dma((4,)), dma((4,)),
-            dma((4,)), dma((4,)),
-            dma((4,)), dma((4,)),
+            dma((16,)), dma((16,)),
             dma((8,)), dma((8,)),
             dma((8,)), dma((8,)),
         ],

time: 115 us -> 91.3 us (0.79)
  Pallas kernels: 112 us -> 88.1 us
    pallas_call x1, Pallas kernels: 112 us -> 88.1 us  [shards(): pl.pallas_call(kernel, out_shape=(jax.ShapeDtypeStruct((4, 128), f32), ja...]
where the time goes in v3:
time: 91.3 us; the launch traced here: 91.1 us
  Pallas kernels  88.1 us (96%)
  local copies, waits for them, and re-layouts  2.36 us (3%)
    pallas_call x1, Pallas kernels, shards(): pl.pallas_call(kernel, out_shape=(jax.ShapeDtypeStruct((4, 128), f32), ja...  88.1 us
    unnamed x9, local copies, waits for them, and re-layouts  2.36 us

profile of v3, /device:TPU:1, one launch (start us, length us, event | category | flops | bytes accessed | tf_op | source)
XLA Modules:
  0.0 91.1 jit_solution(5083734555894010454)
XLA Ops:
  0.6 88.1 %shard_map.76 = (f32[4,128]{1,0:T(4,128)}, f32[1,25]{1,0:T(1,128)}, f32[1,8]{1,0:T(1,128)}) custom-call(s32[8]{0:T(128)} %ranks.1, bf16[512,512]{1,0:T(8,128)(2,1)} %h_in.1, bf16[32,6400]{1,0:T(8,128)(2,1)} %w_in.1, s32[1,512]{1,0:T(1,128)} %bitcast.5, s32[25,1,512]{2,1,0:T(1,128)} %bitcast.4), custom_call_target="tpu_custom_call" | custom-call | tf_op jit(solution)/shard_map/pallas_call | solution.py:430
  88.8 0.0 copy-start
  88.8 0.6 copy-done
  89.4 0.0 copy-start.2
  89.4 0.6 copy.11
  90.0 0.0 copy-done.2
  90.0 0.0 copy-start.1
  90.0 0.5 copy.12
  90.5 0.1 copy-done.1
  90.6 0.5 copy.13
Async XLA Ops:
  88.8 0.7 copy-start
  89.4 0.6 copy-start.2
  90.0 0.6 copy-start.1

commit v4 on v3

--- a/solution.py
+++ b/solution.py
@@ -306,11 +306,11 @@
     unit(1, 0)
     wait_h(6)
     step_z(11)
+    unit(3, 0)
     step_z(12)
     wait_h(7)
     send_h(9)
     step_z(13)
-    unit(3, 0)
     wait_core(2)
     wait_core(3)
     unit(0, 1)
@@ -420,6 +420,17 @@
     lo = jnp.where(none, 0.0, lo)
     q_out[...] = jnp.sum(jnp.where(col == rowi, lo, 0.0), axis=0, keepdims=True)[:, :8]
     drain()
+
+
+def emit(ce_in, mean_in, q_in, ce_out, mean_out, q_out, sem):
+    copies = [
+        pltpu.make_async_copy(src, dst, sem.at[i])
+        for i, (src, dst) in enumerate(((ce_in, ce_out), (mean_in, mean_out), (q_in, q_out)))
+    ]
+    for copy in copies:
+        copy.start()
+    for copy in copies:
+        copy.wait()
 
 
 def shards(hidden, proj_weight, targets, counts, ranks):
@@ -466,7 +477,18 @@
             collective_id=0, has_side_effects=True, vmem_limit_bytes=60 * 2**20
         ),
     )(ranks, hidden, proj_weight, targets.reshape(1, ROWS), counts.transpose(1, 0, 2))
-    return ce.reshape(ROWS), means, quantiles.reshape(8)
+    ce, means, quantiles = pl.pallas_call(
+        emit,
+        out_shape=(
+            jax.ShapeDtypeStruct((ROWS,), f32),
+            jax.ShapeDtypeStruct((1, RES), f32),
+            jax.ShapeDtypeStruct((8,), f32),
+        ),
+        in_specs=[hbm, hbm, hbm],
+        out_specs=(hbm, hbm, hbm),
+        scratch_shapes=[dma((3,))],
+    )(ce.reshape(ROWS), means, quantiles.reshape(8))
+    return ce, means, quantiles
 
 
 def solution(mesh):

time: 91.3 us -> 87.9 us (0.963)
  local copies, waits for them, and re-layouts: 2.36 us -> 0 us
  Pallas kernels: 88.1 us -> 87 us
    unnamed x9 -> x0, local copies, waits for them, and re-layouts: 2.36 us -> none
    pallas_call x1, Pallas kernels: 88.1 us -> 85.8 us  [shards(): pl.pallas_call(kernel, out_shape=(jax.ShapeDtypeStruct((4, 128), f32), ja...]
    pallas_call x0 -> x1, Pallas kernels: none -> 1.22 us  [shards(): pl.pallas_call(emit, out_shape=(jax.ShapeDtypeStruct((ROWS,), f32), jax.S...]
where the time goes in v4:
time: 87.9 us; the launch traced here: 87.8 us
  Pallas kernels  87 us (99%)
    pallas_call x1, Pallas kernels, shards(): pl.pallas_call(kernel, out_shape=(jax.ShapeDtypeStruct((4, 128), f32), ja...  85.8 us

profile of v4, /device:TPU:1, one launch (start us, length us, event | category | flops | bytes accessed | tf_op | source)
XLA Modules:
  0.0 87.8 jit_solution(8250951488778961415)
XLA Ops:
  0.6 85.8 %shard_map.76 = (f32[4,128]{1,0:T(4,128)}, f32[1,25]{1,0:T(1,128)}, f32[1,8]{1,0:T(1,128)}) custom-call(s32[8]{0:T(128)} %ranks.1, bf16[512,512]{1,0:T(8,128)(2,1)} %h_in.1, bf16[32,6400]{1,0:T(8,128)(2,1)} %w_in.1, s32[1,512]{1,0:T(1,128)} %bitcast.5, s32[25,1,512]{2,1,0:T(1,128)} %bitcast.4), custom_call_target="tpu_custom_call" | custom-call | tf_op jit(solution)/shard_map/pallas_call | solution.py:441
  86.4 1.2 %shard_map.77 = (f32[512]{0:T(512)}, f32[1,25]{1,0:T(1,128)}, f32[8]{0:T(128)}) custom-call(f32[512]{0:T(512)} %bitcast.6, f32[1,25]{1,0:T(1,128)} %get-tuple-element.7.mean_in, f32[8]{0:T(128)} %bitcast.7), custom_call_target="tpu_custom_call" | custom-call | tf_op jit(solution)/shard_map/pallas_call | solution.py:480

commit v5 on v4

--- a/solution.py
+++ b/solution.py
@@ -276,11 +276,11 @@
 
     wait_h(0)
     send_h(2)
-    send_h(3)
     step_z(0)
     step_z(1)
     step_z(2)
     wait_h(1)
+    send_h(3)
     send_h(4)
     step_z(3)
     prepare()

time: 87.9 us -> 91 us (1.035)
  Pallas kernels: 87 us -> 90.1 us
    pallas_call x1, Pallas kernels: 85.8 us -> 88.9 us  [shards(): pl.pallas_call(kernel, out_shape=(jax.ShapeDtypeStruct((4, 128), f32), ja...]
where the time goes in v5:
time: 91 us; the launch traced here: 90.9 us
  Pallas kernels  90.1 us (99%)
    pallas_call x1, Pallas kernels, shards(): pl.pallas_call(kernel, out_shape=(jax.ShapeDtypeStruct((4, 128), f32), ja...  88.9 us

profile of v5, /device:TPU:1, one launch (start us, length us, event | category | flops | bytes accessed | tf_op | source)
XLA Modules:
  0.0 90.9 jit_solution(5763391709565386896)
XLA Ops:
  0.6 88.9 %shard_map.76 = (f32[4,128]{1,0:T(4,128)}, f32[1,25]{1,0:T(1,128)}, f32[1,8]{1,0:T(1,128)}) custom-call(s32[8]{0:T(128)} %ranks.1, bf16[512,512]{1,0:T(8,128)(2,1)} %h_in.1, bf16[32,6400]{1,0:T(8,128)(2,1)} %w_in.1, s32[1,512]{1,0:T(1,128)} %bitcast.5, s32[25,1,512]{2,1,0:T(1,128)} %bitcast.4), custom_call_target="tpu_custom_call" | custom-call | tf_op jit(solution)/shard_map/pallas_call | solution.py:441
  89.5 1.2 %shard_map.77 = (f32[512]{0:T(512)}, f32[1,25]{1,0:T(1,128)}, f32[8]{0:T(128)}) custom-call(f32[512]{0:T(512)} %bitcast.6, f32[1,25]{1,0:T(1,128)} %get-tuple-element.7.mean_in, f32[8]{0:T(128)} %bitcast.7), custom_call_target="tpu_custom_call" | custom-call | tf_op jit(solution)/shard_map/pallas_call | solution.py:480
